TPU v7x, 512 devices: a whole 4x4x16 slice. The times are simulated.
512 devices in a mesh: sta: 16 (over x_lo, y, core), src: 32 (over z, x_hi).
Axes of the slice: x: 4 (x_hi: 2, x_lo: 2; x = x_hi * 2 + x_lo), y: 4, z: 16, core: 2. Of those that a mesh axis runs over, the one named last changes fastest.
Arguments:
- features: bfloat16 [512, 1024, 128], P('sta', 'src'), may hold values from -6 to 6
- station_lists: int32 [512, 16], replicated, may hold values from 0 to 511, as said below
- station_counts: int32 [512], replicated, may hold values from 1 to 16
- source_lists: int32 [1024, 16], replicated, may hold values from 0 to 1023, as said below
- source_counts: int32 [1024], replicated, may hold values from 1 to 16
- picks: int32 [2, 512], P(None, 'sta'), may hold values 0 or 1
- targets: float32 [2, 1024], P(None, 'src'), may hold values from 0 to 1
- layer_weights: bfloat16 [2, 3, 64, 64], replicated, may hold values from -0.75 to 0.75
- readout_vector: bfloat16 [64], replicated, may hold values from -0.75 to 0.75
Outputs:
- likelihood: float32 [2, 1024], P(None, 'src')
- feature_grad: bfloat16 [512, 1024, 128], P('sta', 'src')
- weight_grad: float32 [2, 3, 64, 64], replicated
- vector_grad: float32 [64], replicated
Inputs may be any that keep to these rules, and one draw needn't show every extreme that they name: `station_lists`: every entry of a station's list lies within 16 rows of that station; entries past its count are padding. `source_lists`: every entry of a source node's list lies within 16 rows of that source node; entries past its count are padding.
All inputs are finite; a program needn't handle non-finite values. No bound on the sum of `picks` on one device may be relied on, other than what follows from the above.
Results may differ from a plain program's by a relative error of at most 0.015.
Values may be sent and summed in bfloat16 or wider, within the bound.
No kernel may reach another device: no remote copies, remote signals or barrier semaphores. Data moves between devices by JAX's collectives and lax.ppermute only.
A program may use at most 64 MiB of HBM per device.

v0:
```python
import jax
import jax.numpy as jnp
from jax import lax
from jax.sharding import PartitionSpec as P

LAYERS = 2
HW = 16


def padded_2(cells, sides, width):
    for axis, dim in sides:
        count = lax.axis_size(axis)
        ends = count - 1
        head = lax.slice_in_dim(cells, 0, width, axis=dim)
        tail = lax.slice_in_dim(cells, cells.shape[dim] - width, cells.shape[dim], axis=dim)
        cells = jnp.concatenate(
            [
                lax.ppermute(tail, axis, [(i, (i + 1) % count) for i in range(ends)]),
                cells,
                lax.ppermute(head, axis, [((i + 1) % count, i) for i in range(ends)]),
            ],
            axis=dim,
        )
    return cells


def count_matrix(lists, counts, first_row, span):
    list_width = lists.shape[1]
    in_list = jnp.arange(list_width)[None, :] < counts[:, None]
    shifted = lists - first_row
    matches = (shifted[:, :, None] == jnp.arange(span)[None, None, :]) & in_list[:, :, None]
    return jnp.sum(matches.astype(jnp.float32), axis=1).astype(jnp.bfloat16)


def blocked(matrix, windows):
    return jnp.kron(jnp.eye(windows, dtype=jnp.bfloat16), matrix)


def apply_block(values, matrix):
    channels = values.shape[-1]
    flat = values.reshape(-1, channels)
    return jnp.dot(flat, matrix, preferred_element_type=jnp.float32).reshape(values.shape)


def outer_sum(left, right, feature):
    return jnp.einsum(
        "nf,ng->fg",
        left.reshape(-1, feature),
        right.reshape(-1, feature),
        preferred_element_type=jnp.float32,
    )


def shards(
    features,
    station_lists,
    station_counts,
    source_lists,
    source_counts,
    picks,
    targets,
    layer_weights,
    readout_vector,
):
    sta_rows, src_rows, channels = features.shape
    feature = layer_weights.shape[-1]
    windows = channels // feature
    sta_first = lax.axis_index("sta") * sta_rows
    src_first = lax.axis_index("src") * src_rows
    own_slists = lax.dynamic_slice_in_dim(station_lists, sta_first, sta_rows, 0)
    own_scounts = lax.dynamic_slice_in_dim(station_counts, sta_first, sta_rows, 0)
    own_rlists = lax.dynamic_slice_in_dim(source_lists, src_first, src_rows, 0)
    own_rcounts = lax.dynamic_slice_in_dim(source_counts, src_first, src_rows, 0)
    sta_mix = count_matrix(own_slists, own_scounts, sta_first - HW, sta_rows + 2 * HW)
    src_mix = count_matrix(own_rlists, own_rcounts, src_first - HW, src_rows + 2 * HW)
    sta_div = own_scounts.astype(jnp.float32)[:, None, None]
    src_div = own_rcounts.astype(jnp.float32)[None, :, None]
    blocks = [
        [blocked(layer_weights[layer_idx, which], windows) for which in range(3)]
        for layer_idx in range(LAYERS)
    ]
    states = features
    saved = []
    for layer_idx in range(LAYERS):
        padded = padded_2(states, (("sta", 0), ("src", 1)), HW)
        along_sta = jnp.einsum(
            "im,mjc->ijc",
            sta_mix,
            padded[:, HW : HW + src_rows],
            preferred_element_type=jnp.float32,
        )
        sta_mean = (along_sta / sta_div).astype(jnp.bfloat16)
        along_src = jnp.einsum(
            "jm,imc->ijc", src_mix, padded[HW : HW + sta_rows], preferred_element_type=jnp.float32
        )
        src_mean = (along_src / src_div).astype(jnp.bfloat16)
        linear = (
            apply_block(states, blocks[layer_idx][0])
            + apply_block(sta_mean, blocks[layer_idx][1])
            + apply_block(src_mean, blocks[layer_idx][2])
        )
        squashed = jnp.tanh(linear)
        saved.append((states, sta_mean, src_mean, squashed))
        states = (states.astype(jnp.float32) + squashed).astype(jnp.bfloat16)
    vector_cols = (
        jnp.eye(windows, dtype=jnp.bfloat16)[:, None, :] * readout_vector[None, :, None]
    ).reshape(channels, windows)
    score = jnp.dot(
        states.reshape(-1, channels), vector_cols, preferred_element_type=jnp.float32
    ).reshape(sta_rows, src_rows, windows)
    picked = picks.astype(jnp.float32)
    partial_sum = jnp.sum(picked.T[:, None, :] * score, axis=0).T
    local_count = jnp.sum(picked, axis=1)
    summed, count = lax.psum((partial_sum, local_count), "sta")
    root = jnp.sqrt(jnp.maximum(count, 1.0))
    likelihood = summed / root[:, None]
    error = jax.nn.sigmoid(likelihood) - targets
    d_score = (picked.T[:, None, :] * error.T[None, :, :]).astype(jnp.bfloat16)
    v_sum = jnp.einsum(
        "nw,nwf->f",
        d_score.reshape(-1, windows),
        states.reshape(-1, windows, feature),
        preferred_element_type=jnp.float32,
    )
    grad = (d_score.astype(jnp.float32)[..., None] * readout_vector.astype(jnp.float32)).reshape(
        sta_rows, src_rows, channels
    )
    w_rows = []
    for layer_idx in reversed(range(LAYERS)):
        before, sta_mean, src_mean, squashed = saved[layer_idx]
        delta = (grad * (1.0 - squashed * squashed)).astype(jnp.bfloat16)
        w_rows.append(
            jnp.stack(
                [
                    outer_sum(before, delta, feature),
                    outer_sum(sta_mean, delta, feature),
                    outer_sum(src_mean, delta, feature),
                ]
            )
        )
        u_sta = (apply_block(delta, blocks[layer_idx][1].T) / sta_div).astype(jnp.bfloat16)
        u_src = (apply_block(delta, blocks[layer_idx][2].T) / src_div).astype(jnp.bfloat16)
        direct = grad + apply_block(delta, blocks[layer_idx][0].T)
        spread_sta = jnp.einsum("im,ijc->mjc", sta_mix, u_sta, preferred_element_type=jnp.float32)
        rim_rows = jnp.concatenate([spread_sta[:HW], spread_sta[sta_rows + HW :]], 0)
        got_rows = padded_2(rim_rows.astype(jnp.bfloat16), (("sta", 0),), HW).astype(rim_rows.dtype)
        from_sta = spread_sta[HW : sta_rows + HW]
        from_sta = from_sta + jnp.pad(got_rows[:HW], ((0, sta_rows - HW), (0, 0), (0, 0)))
        from_sta = from_sta + jnp.pad(got_rows[3 * HW :], ((sta_rows - HW, 0), (0, 0), (0, 0)))
        spread_src = jnp.einsum("jm,ijc->imc", src_mix, u_src, preferred_element_type=jnp.float32)
        rim_cols = jnp.concatenate([spread_src[:, :HW], spread_src[:, src_rows + HW :]], 1)
        got_cols = padded_2(rim_cols.astype(jnp.bfloat16), (("src", 1),), HW).astype(rim_cols.dtype)
        from_src = spread_src[:, HW : src_rows + HW]
        from_src = from_src + jnp.pad(got_cols[:, :HW], ((0, 0), (0, src_rows - HW), (0, 0)))
        from_src = from_src + jnp.pad(got_cols[:, 3 * HW :], ((0, 0), (src_rows - HW, 0), (0, 0)))
        grad = direct + from_sta + from_src
    w_sum = jnp.stack(w_rows[::-1])
    w_total, v_total = lax.psum((w_sum, v_sum), ("sta", "src"))
    node_total = jnp.float32(sta_rows * lax.axis_size("sta")) * jnp.float32(
        src_rows * lax.axis_size("src")
    )
    factor = 1.0 / jnp.sqrt(node_total)
    return (likelihood, grad.astype(jnp.bfloat16), w_total * factor, v_total * factor)


def solution(mesh):
    in_specs = (P("sta", "src", None), P(), P(), P(), P(), P(None, "sta"), P(None, "src"), P(), P())
    out_specs = (P(None, "src"), P("sta", "src", None), P(), P())
    return jax.shard_map(shards, mesh=mesh, in_specs=in_specs, out_specs=out_specs, check_vma=False)
```

profile of v0, /device:TPU:1, one launch (start us, length us, event | category | flops | bytes accessed | tf_op | source)
XLA Modules:
  0.0 722.8 jit_solution(12138712805420795126)
XLA Ops:
  8.3 4.6 collective-permute-start
  12.9 5.5 collective-permute-start.1
  19.1 1.2 fusion.59
  20.5 1.3 fusion.60
  31.4 1.3 collective-permute-start.2
  32.7 1.3 collective-permute-start.3
  36.4 7.6 %collective-permute-done.2 = bf16[64,16,128]{2,0,1:T(8,128)(2,1)S(1)} collective-permute-done((bf16[64,16,128]{2,0,1:T(8,128)(2,1)S(1)}, bf16[64,16,128]{2,0,1:T(8,128)(2,1)S(1)}, u32[]{:S(2)}, u32[]{:S(2)}) %collective-permute-start.2) | collective-permute-done | bytes 262176 | tf_op jit(solution)/shard_map/ppermute | solution.py:18
  48.2 3.6 collective-permute-start.4
  51.8 1.9 collective-permute-start.5
  53.9 4.1 collective-permute-done.5
  58.2 5.6 collective-permute-start.6
  63.8 1.3 collective-permute-start.7
  65.5 1.1 reshape.268
  67.3 5.6 collective-permute-done.7
  74.5 1.1 reshape.270
  76.8 25.8 %all-reduce.4 = (f32[2,32]{1,0:T(2,128)S(1)}, f32[2]{0:T(128)S(1)}) all-reduce(f32[2,32]{1,0:T(2,128)S(1)} %bitcast.115, f32[2]{0:T(128)S(1)} %copy-done.40), channel_id=1, replica_groups=mesh['sta'=16,'src'=32] {'sta'}, use_global_device_ids=true, to_apply=%region_3.4 | all-reduce | flops 66 | bytes 528 | tf_op jit(solution)/shard_map/psum | solution.py:114
  104.9 1.2 mul.284
  108.7 1.4 copy.149
  110.7 2.4 fusion.69
  113.4 115.2 %psum.31 = f32[64]{0:T(128)S(1)} all-reduce(f32[64]{0:T(128)S(1)} %convolution_bitcast_fusion.9), channel_id=1, replica_groups=mesh['sta'=16,'src'=32] {'sta','src'}, use_global_device_ids=true, to_apply=%region_7.8 | all-reduce | flops 64 | bytes 512 | tf_op jit(solution)/shard_map/psum | solution.py:158
  231.3 2.9 collective-permute-start.8
  234.2 1.9 collective-permute-start.9
  236.2 3.5 collective-permute-start.10
  239.6 1.5 collective-permute-start.11
  242.2 5.4 collective-permute-done.11
  248.7 1.2 multiply_convert_fusion
  252.4 1.7 fusion.70
  257.7 4.3 collective-permute-start.12
  262.0 1.9 collective-permute-start.13
  264.0 4.2 collective-permute-start.14
  268.2 1.3 collective-permute-start.15
  269.5 442.2 %all-reduce.7.cloned.1.call-done = f32[2,3,64,64]{2,3,1,0:T(8,128)} async-done(((f32[2,3,64,64]{2,3,1,0:T(8,128)}), f32[2,3,64,64]{2,3,1,0:T(8,128)}) %all-reduce.7.cloned.1.call-update) | async-done | bytes 98320 | tf_op jit(solution)/shard_map/psum | solution.py:158
  (193 shorter events, 42.8 us)
Async XLA Ops:
  7.2 704.5 %all-reduce.7.cloned.1.call-start = ((), (), s32[]{:S(2)}) async-start(), calls=%async_computation | async-start | bytes 393216 | tf_op jit(solution)/shard_map/psum | solution.py:158
  8.3 22.9 %collective-permute-start = (bf16[16,32,128]{2,0,1:T(8,128)(2,1)S(1)}, bf16[16,32,128]{2,0,1:T(8,128)(2,1)S(1)}, u32[]{:S(2)}, u32[]{:S(2)}) collective-permute-start(bf16[16,32,128]{2,0,1:T(8,128)(2,1)S(1)} %copy.146), channel_id=1, source_target_pairs={{0,32},{32,64},{64,96},{96,128},{128,160},{160,192},{192,224},{224... | collective-permute-start | bytes 393224 | tf_op jit(solution)/shard_map/ppermute | solution.py:18
  12.9 9.9 %copy-start.19 = (bf16[2,3,64,64]{3,2,1,0:T(8,128)(2,1)S(1)}, bf16[2,3,64,64]{3,2,1,0:T(8,128)(2,1)}, u32[]{:S(2)}) copy-start(bf16[2,3,64,64]{3,2,1,0:T(8,128)(2,1)} %param.16) | copy-start | bytes 147460
  12.9 18.4 %collective-permute-start.1 = (bf16[16,32,128]{2,0,1:T(8,128)(2,1)S(1)}, bf16[16,32,128]{2,0,1:T(8,128)(2,1)S(1)}, u32[]{:S(2)}, u32[]{:S(2)}) collective-permute-start(bf16[16,32,128]{2,0,1:T(8,128)(2,1)S(1)} %copy.147), channel_id=1, source_target_pairs={{32,0},{64,32},{96,64},{128,96},{160,128},{192,160},{224,192},{256... | collective-permute-start | bytes 393224 | tf_op jit(solution)/shard_map/ppermute | solution.py:20
  19.1 56.8 %copy-start.20 = (f32[32,2]{0,1:T(2,128)}, f32[32,2]{0,1:T(2,128)S(1)}, u32[]{:S(2)}) copy-start(f32[32,2]{0,1:T(2,128)S(1)} %convert_bitcast_fusion) | copy-start | bytes 772
  22.7 1.5 copy-start
  24.2 40.9 %copy-start.22 = (bf16[32,64]{1,0:T(8,128)(2,1)}, bf16[32,64]{1,0:T(8,128)(2,1)S(1)}, u32[]{:S(2)}) copy-start(bf16[32,64]{1,0:T(8,128)(2,1)S(1)} %convert_reduce_fusion.1) | copy-start | bytes 12292
  31.4 12.6 %collective-permute-start.2 = (bf16[64,16,128]{2,0,1:T(8,128)(2,1)S(1)}, bf16[64,16,128]{2,0,1:T(8,128)(2,1)S(1)}, u32[]{:S(2)}, u32[]{:S(2)}) collective-permute-start(bf16[64,16,128]{2,0,1:T(8,128)(2,1)S(1)} %get-tuple-element.38), channel_id=1, source_target_pairs={{0,1},{1,2},{2,3},{3,4},{4,5},{5,6},{6,7},{7,8},{8,9},{9,10},{10,1... | collective-permute-start | bytes 786440 | tf_op jit(solution)/shard_map/ppermute | solution.py:18
  32.7 1.3 copy-start.36
  32.7 11.4 %collective-permute-start.3 = (bf16[64,16,128]{2,0,1:T(8,128)(2,1)S(1)}, bf16[64,16,128]{2,0,1:T(8,128)(2,1)S(1)}, u32[]{:S(2)}, u32[]{:S(2)}) collective-permute-start(bf16[64,16,128]{2,0,1:T(8,128)(2,1)S(1)} %get-tuple-element.39), channel_id=1, source_target_pairs={{1,0},{2,1},{3,2},{4,3},{5,4},{6,5},{7,6},{8,7},{9,8},{10,9},{11,1... | collective-permute-start | bytes 786440 | tf_op jit(solution)/shard_map/ppermute | solution.py:20
  36.4 7.8 %copy-start.25 = (bf16[32,64]{1,0:T(8,128)(2,1)S(1)}, bf16[32,64]{1,0:T(8,128)(2,1)}, u32[]{:S(2)}) copy-start(bf16[32,64]{1,0:T(8,128)(2,1)} %convert_reduce_fusion) | copy-start | bytes 12292
  48.2 5.7 collective-permute-start.4
  51.8 6.3 collective-permute-start.5
  58.2 6.9 copy-start.37
  58.2 9.1 %collective-permute-start.6 = (bf16[64,16,128]{2,1,0:T(8,128)(2,1)S(1)}, bf16[64,16,128]{2,1,0:T(8,128)(2,1)S(1)}, u32[]{:S(2)}, u32[]{:S(2)}) collective-permute-start(bf16[64,16,128]{2,1,0:T(8,128)(2,1)S(1)} %get-tuple-element.36), channel_id=1, source_target_pairs={{0,1},{1,2},{2,3},{3,4},{4,5},{5,6},{6,7},{7,8},{8,9},{9,10},{10,1... | collective-permute-start | bytes 786440 | tf_op jit(solution)/shard_map/ppermute | solution.py:18
  63.8 9.1 %collective-permute-start.7 = (bf16[64,16,128]{2,1,0:T(8,128)(2,1)S(1)}, bf16[64,16,128]{2,1,0:T(8,128)(2,1)S(1)}, u32[]{:S(2)}, u32[]{:S(2)}) collective-permute-start(bf16[64,16,128]{2,1,0:T(8,128)(2,1)S(1)} %get-tuple-element.37), channel_id=1, source_target_pairs={{1,0},{2,1},{3,2},{4,3},{5,4},{6,5},{7,6},{8,7},{9,8},{10,9},{11,1... | collective-permute-start | bytes 786440 | tf_op jit(solution)/shard_map/ppermute | solution.py:20
  66.6 6.3 copy-start.26
  110.7 2.5 copy-start.1
  113.1 116.0 %copy-start.7 = (bf16[2048,64]{1,0:T(8,128)(2,1)S(1)}, bf16[2048,64]{1,0:T(8,128)(2,1)}, u32[]{:S(2)}) copy-start(bf16[2048,64]{1,0:T(8,128)(2,1)} %reshape.269) | copy-start | bytes 786436
  230.2 5.9 copy-start.16
  231.2 9.9 %copy-start.5 = (bf16[2048,64]{1,0:T(8,128)(2,1)S(1)}, bf16[2048,64]{1,0:T(8,128)(2,1)}, u32[]{:S(2)}) copy-start(bf16[2048,64]{1,0:T(8,128)(2,1)} %reshape.266) | copy-start | bytes 786436
  231.3 10.8 %collective-permute-start.8 = (bf16[16,32,128]{2,1,0:T(8,128)(2,1)S(1)}, bf16[16,32,128]{2,1,0:T(8,128)(2,1)S(1)}, u32[]{:S(2)}, u32[]{:S(2)}) collective-permute-start(bf16[16,32,128]{2,1,0:T(8,128)(2,1)S(1)} %get-tuple-element.32), channel_id=1, source_target_pairs={{0,32},{32,64},{64,96},{96,128},{128,160},{160,192},{192,224},{224... | collective-permute-start | bytes 393224 | tf_op jit(solution)/shard_map/ppermute | solution.py:18
  234.2 7.9 %collective-permute-start.9 = (bf16[16,32,128]{2,1,0:T(8,128)(2,1)S(1)}, bf16[16,32,128]{2,1,0:T(8,128)(2,1)S(1)}, u32[]{:S(2)}, u32[]{:S(2)}) collective-permute-start(bf16[16,32,128]{2,1,0:T(8,128)(2,1)S(1)} %get-tuple-element.33), channel_id=1, source_target_pairs={{32,0},{64,32},{96,64},{128,96},{160,128},{192,160},{224,192},{256... | collective-permute-start | bytes 393224 | tf_op jit(solution)/shard_map/ppermute | solution.py:20
  236.2 6.0 collective-permute-start.10
  239.6 8.0 %collective-permute-start.11 = (bf16[32,16,128]{2,1,0:T(8,128)(2,1)S(1)}, bf16[32,16,128]{2,1,0:T(8,128)(2,1)S(1)}, u32[]{:S(2)}, u32[]{:S(2)}) collective-permute-start(bf16[32,16,128]{2,1,0:T(8,128)(2,1)S(1)} %get-tuple-element.35), channel_id=1, source_target_pairs={{1,0},{2,1},{3,2},{4,3},{5,4},{6,5},{7,6},{8,7},{9,8},{10,9},{11,1... | collective-permute-start | bytes 393224 | tf_op jit(solution)/shard_map/ppermute | solution.py:20
  242.2 5.6 copy-start.12
  252.4 1.7 copy-start.4
  257.0 7.0 copy-start.15
  257.7 455.7 %collective-permute-start.12 = (bf16[16,32,128]{2,1,0:T(8,128)(2,1)S(1)}, bf16[16,32,128]{2,1,0:T(8,128)(2,1)S(1)}, u32[]{:S(2)}, u32[]{:S(2)}) collective-permute-start(bf16[16,32,128]{2,1,0:T(8,128)(2,1)S(1)} %get-tuple-element.28), channel_id=1, source_target_pairs={{0,32},{32,64},{64,96},{96,128},{128,160},{160,192},{192,224},{224... | collective-permute-start | bytes 393224 | tf_op jit(solution)/shard_map/ppermute | solution.py:18
  262.0 451.4 %collective-permute-start.13 = (bf16[16,32,128]{2,1,0:T(8,128)(2,1)S(1)}, bf16[16,32,128]{2,1,0:T(8,128)(2,1)S(1)}, u32[]{:S(2)}, u32[]{:S(2)}) collective-permute-start(bf16[16,32,128]{2,1,0:T(8,128)(2,1)S(1)} %get-tuple-element.29), channel_id=1, source_target_pairs={{32,0},{64,32},{96,64},{128,96},{160,128},{192,160},{224,192},{256... | collective-permute-start | bytes 393224 | tf_op jit(solution)/shard_map/ppermute | solution.py:20
  264.0 449.6 %collective-permute-start.14 = (bf16[32,16,128]{2,1,0:T(8,128)(2,1)S(1)}, bf16[32,16,128]{2,1,0:T(8,128)(2,1)S(1)}, u32[]{:S(2)}, u32[]{:S(2)}) collective-permute-start(bf16[32,16,128]{2,1,0:T(8,128)(2,1)S(1)} %get-tuple-element.30), channel_id=1, source_target_pairs={{0,1},{1,2},{2,3},{3,4},{4,5},{5,6},{6,7},{7,8},{8,9},{9,10},{10,1... | collective-permute-start | bytes 393224 | tf_op jit(solution)/shard_map/ppermute | solution.py:18
  268.2 445.4 %collective-permute-start.15 = (bf16[32,16,128]{2,1,0:T(8,128)(2,1)S(1)}, bf16[32,16,128]{2,1,0:T(8,128)(2,1)S(1)}, u32[]{:S(2)}, u32[]{:S(2)}) collective-permute-start(bf16[32,16,128]{2,1,0:T(8,128)(2,1)S(1)} %get-tuple-element.31), channel_id=1, source_target_pairs={{1,0},{2,1},{3,2},{4,3},{5,4},{6,5},{7,6},{8,7},{9,8},{10,9},{11,1... | collective-permute-start | bytes 393224 | tf_op jit(solution)/shard_map/ppermute | solution.py:20
  (26 other events, 22.2 us)
Sparse Core Ops, SparseCore 0:
  257.8 453.8 all-reduce.6
where the time goes:
time: 724 us; the launch traced here: 723 us
  waiting for transfers between devices  466 us (64%)
  blocking collectives  141 us (19%)
  starting transfers between devices  46.6 us (6%)
  local copies, waits for them, and re-layouts  29.8 us (4%)
  matrix products  14.8 us (2%)
  between operations  14.8 us (2%)
  other arithmetic  10.1 us (1%)
    psum x1, waiting for transfers between devices, shards(): w_total, v_total = lax.psum((w_sum, v_sum), ('sta', 'src'))  442 us
    psum x1, blocking collectives, shards(): w_total, v_total = lax.psum((w_sum, v_sum), ('sta', 'src'))  115 us
    ppermute x8, starting transfers between devices, padded_2(): lax.ppermute(tail, axis, [(i, (i + 1) % count) for i in range(ends)])  30 us
    psum x1, blocking collectives, shards(): summed, count = lax.psum((partial_sum, local_count), 'sta')  25.8 us
    ppermute x8, starting transfers between devices, padded_2(): lax.ppermute(head, axis, [((i + 1) % count, i) for i in range(ends)])  16.6 us
    ppermute x8, waiting for transfers between devices, padded_2(): lax.ppermute(head, axis, [((i + 1) % count, i) for i in range(ends)])  15.3 us
  transfers between devices with their start and end apart: 17, of which 7 were waited for; matrix products, arithmetic and copies ran while one was open for 3% of the time, Pallas kernels for 0%

commit v1 on v0

--- a/solution.py
+++ b/solution.py
@@ -2,6 +2,7 @@
 import jax.numpy as jnp
 from jax import lax
 from jax.sharding import PartitionSpec as P
+from jax.lax import psum
 
 LAYERS = 2
 HW = 16
@@ -155,7 +156,8 @@
         from_src = from_src + jnp.pad(got_cols[:, 3 * HW :], ((0, 0), (src_rows - HW, 0), (0, 0)))
         grad = direct + from_sta + from_src
     w_sum = jnp.stack(w_rows[::-1])
-    w_total, v_total = lax.psum((w_sum, v_sum), ("sta", "src"))
+    _build_edge = lambda payload: psum(psum(payload, axis_name="src"), axis_name="sta")
+    w_total, v_total = _build_edge((w_sum, v_sum))
     node_total = jnp.float32(sta_rows * lax.axis_size("sta")) * jnp.float32(
         src_rows * lax.axis_size("src")
     )

time: 724 us -> 698 us (0.964)
  waiting for transfers between devices: 466 us -> 444 us
    psum x1 -> x2, waiting for transfers between devices: 442 us -> 420 us  [the longest x1 276 us: shards(): psum(payload, axis_name='src')]
    psum x1 -> x2, blocking collectives: 115 us -> 113 us  [the longest x1 70.4 us: shards(): psum(payload, axis_name='src')]
  transfers between devices with their start and end apart: 17 -> 18, of which waited for: 7 -> 9; matrix products, arithmetic and copies ran while one was open for 3% -> 3% of each run, Pallas kernels for 0% -> 0%
where the time goes in v1:
time: 698 us; the launch traced here: 697 us
  waiting for transfers between devices  444 us (64%)
  blocking collectives  139 us (20%)
  starting transfers between devices  43.9 us (6%)
  local copies, waits for them, and re-layouts  30 us (4%)
  matrix products  14.8 us (2%)
  between operations  14.8 us (2%)
  other arithmetic  10.1 us (1%)
    psum x1, waiting for transfers between devices, shards(): psum(payload, axis_name='src')  276 us
    psum x1, waiting for transfers between devices, shards(): psum(psum(payload, axis_name='src'), axis_name='sta')  144 us
    psum x1, blocking collectives, shards(): psum(payload, axis_name='src')  70.4 us
    psum x1, blocking collectives, shards(): psum(psum(payload, axis_name='src'), axis_name='sta')  42.6 us
    ppermute x8, starting transfers between devices, padded_2(): lax.ppermute(tail, axis, [(i, (i + 1) % count) for i in range(ends)])  26.8 us
    psum x1, blocking collectives, shards(): summed, count = lax.psum((partial_sum, local_count), 'sta')  25.8 us
    ppermute x8, starting transfers between devices, padded_2(): lax.ppermute(head, axis, [((i + 1) % count, i) for i in range(ends)])  17.1 us
    ppermute x8, waiting for transfers between devices, padded_2(): lax.ppermute(head, axis, [((i + 1) % count, i) for i in range(ends)])  15.5 us
  transfers between devices with their start and end apart: 18, of which 9 were waited for; matrix products, arithmetic and copies ran while one was open for 3% of the time, Pallas kernels for 0%

profile of v1, /device:TPU:1, one launch (start us, length us, event | category | flops | bytes accessed | tf_op | source)
XLA Modules:
  0.0 696.6 jit_solution(3448681736930924643)
XLA Ops:
  8.3 4.6 collective-permute-start
  12.9 5.5 collective-permute-start.1
  19.1 1.3 fusion.59
  20.5 1.3 fusion.60
  31.5 1.3 collective-permute-start.2
  32.8 1.3 collective-permute-start.3
  36.5 7.6 %collective-permute-done.2 = bf16[64,16,128]{2,0,1:T(8,128)(2,1)S(1)} collective-permute-done((bf16[64,16,128]{2,0,1:T(8,128)(2,1)S(1)}, bf16[64,16,128]{2,0,1:T(8,128)(2,1)S(1)}, u32[]{:S(2)}, u32[]{:S(2)}) %collective-permute-start.2) | collective-permute-done | bytes 262176 | tf_op jit(solution)/shard_map/ppermute | solution.py:19
  48.3 3.6 collective-permute-start.4
  51.9 1.9 collective-permute-start.5
  54.1 4.1 collective-permute-done.5
  58.3 5.6 collective-permute-start.6
  63.9 1.3 collective-permute-start.7
  67.5 5.6 collective-permute-done.7
  76.9 25.8 %all-reduce.4 = (f32[2,32]{1,0:T(2,128)S(1)}, f32[2]{0:T(128)S(1)}) all-reduce(f32[2,32]{1,0:T(2,128)S(1)} %bitcast.115, f32[2]{0:T(128)S(1)} %copy-done.40), channel_id=1, replica_groups=mesh['sta'=16,'src'=32] {'sta'}, use_global_device_ids=true, to_apply=%region_3.4 | all-reduce | flops 66 | bytes 528 | tf_op jit(solution)/shard_map/psum | solution.py:115
  105.1 1.2 mul.284
  108.8 1.4 copy.149
  110.8 2.4 fusion.69
  113.5 70.4 %psum.46 = f32[64]{0:T(128)S(1)} all-reduce(f32[64]{0:T(128)S(1)} %convolution_bitcast_fusion.9), channel_id=1, replica_groups=mesh['sta'=16,'src'=32] {'src'}, use_global_device_ids=true, to_apply=%region_8.9 | all-reduce | flops 64 | bytes 512 | tf_op jit(solution)/shard_map/psum | solution.py:159
  183.9 42.6 %psum.47 = f32[64]{0:T(128)S(1)} all-reduce(f32[64]{0:T(128)S(1)} %psum.46), channel_id=1, replica_groups=mesh['sta'=16,'src'=32] {'sta'}, use_global_device_ids=true, to_apply=%region_9.10 | all-reduce | flops 64 | bytes 512 | tf_op jit(solution)/shard_map/psum | solution.py:159
  229.2 2.1 collective-permute-start.8
  231.3 2.4 collective-permute-start.9
  233.7 2.9 collective-permute-start.10
  236.6 1.5 collective-permute-start.11
  239.8 5.6 collective-permute-done.11
  246.5 1.1 multiply_convert_fusion
  249.1 1.7 fusion.70
  255.1 3.1 collective-permute-start.12
  258.2 1.9 collective-permute-start.13
  260.8 3.6 collective-permute-start.14
  264.4 1.3 collective-permute-start.15
  265.7 275.6 %all-reduce.8.cloned.1.call-done = f32[2,3,64,64]{2,3,1,0:T(8,128)} async-done(((f32[2,3,64,64]{2,3,1,0:T(8,128)}), f32[2,3,64,64]{2,3,1,0:T(8,128)}) %all-reduce.8.cloned.1.call-update) | async-done | bytes 98320 | tf_op jit(solution)/shard_map/psum | solution.py:159
  543.8 144.2 %all-reduce.10.cloned.1.call-done = f32[2,3,64,64]{2,3,1,0:T(8,128)} async-done(((f32[2,3,64,64]{2,3,1,0:T(8,128)}), f32[2,3,64,64]{2,3,1,0:T(8,128)}) %all-reduce.10.cloned.1.call-update) | async-done | bytes 98320 | tf_op jit(solution)/shard_map/psum | solution.py:159
  (197 shorter events, 45.8 us)
Async XLA Ops:
  7.2 534.1 %all-reduce.8.cloned.1.call-start = ((), (), s32[]{:S(2)}) async-start(), calls=%async_computation | async-start | bytes 393216 | tf_op jit(solution)/shard_map/psum | solution.py:159
  8.3 23.0 %collective-permute-start = (bf16[16,32,128]{2,0,1:T(8,128)(2,1)S(1)}, bf16[16,32,128]{2,0,1:T(8,128)(2,1)S(1)}, u32[]{:S(2)}, u32[]{:S(2)}) collective-permute-start(bf16[16,32,128]{2,0,1:T(8,128)(2,1)S(1)} %copy.146), channel_id=1, source_target_pairs={{0,32},{32,64},{64,96},{96,128},{128,160},{160,192},{192,224},{224... | collective-permute-start | bytes 393224 | tf_op jit(solution)/shard_map/ppermute | solution.py:19
  12.9 9.9 %copy-start.19 = (bf16[2,3,64,64]{3,2,1,0:T(8,128)(2,1)S(1)}, bf16[2,3,64,64]{3,2,1,0:T(8,128)(2,1)}, u32[]{:S(2)}) copy-start(bf16[2,3,64,64]{3,2,1,0:T(8,128)(2,1)} %param.16) | copy-start | bytes 147460
  12.9 18.5 %collective-permute-start.1 = (bf16[16,32,128]{2,0,1:T(8,128)(2,1)S(1)}, bf16[16,32,128]{2,0,1:T(8,128)(2,1)S(1)}, u32[]{:S(2)}, u32[]{:S(2)}) collective-permute-start(bf16[16,32,128]{2,0,1:T(8,128)(2,1)S(1)} %copy.147), channel_id=1, source_target_pairs={{32,0},{64,32},{96,64},{128,96},{160,128},{192,160},{224,192},{256... | collective-permute-start | bytes 393224 | tf_op jit(solution)/shard_map/ppermute | solution.py:21
  19.1 57.0 %copy-start.20 = (f32[32,2]{0,1:T(2,128)}, f32[32,2]{0,1:T(2,128)S(1)}, u32[]{:S(2)}) copy-start(f32[32,2]{0,1:T(2,128)S(1)} %convert_bitcast_fusion) | copy-start | bytes 772
  22.8 1.5 copy-start
  24.3 40.9 %copy-start.22 = (bf16[32,64]{1,0:T(8,128)(2,1)}, bf16[32,64]{1,0:T(8,128)(2,1)S(1)}, u32[]{:S(2)}) copy-start(bf16[32,64]{1,0:T(8,128)(2,1)S(1)} %convert_reduce_fusion.1) | copy-start | bytes 12292
  31.5 12.6 %collective-permute-start.2 = (bf16[64,16,128]{2,0,1:T(8,128)(2,1)S(1)}, bf16[64,16,128]{2,0,1:T(8,128)(2,1)S(1)}, u32[]{:S(2)}, u32[]{:S(2)}) collective-permute-start(bf16[64,16,128]{2,0,1:T(8,128)(2,1)S(1)} %get-tuple-element.38), channel_id=1, source_target_pairs={{0,1},{1,2},{2,3},{3,4},{4,5},{5,6},{6,7},{7,8},{8,9},{9,10},{10,1... | collective-permute-start | bytes 786440 | tf_op jit(solution)/shard_map/ppermute | solution.py:19
  32.8 11.4 %collective-permute-start.3 = (bf16[64,16,128]{2,0,1:T(8,128)(2,1)S(1)}, bf16[64,16,128]{2,0,1:T(8,128)(2,1)S(1)}, u32[]{:S(2)}, u32[]{:S(2)}) collective-permute-start(bf16[64,16,128]{2,0,1:T(8,128)(2,1)S(1)} %get-tuple-element.39), channel_id=1, source_target_pairs={{1,0},{2,1},{3,2},{4,3},{5,4},{6,5},{7,6},{8,7},{9,8},{10,9},{11,1... | collective-permute-start | bytes 786440 | tf_op jit(solution)/shard_map/ppermute | solution.py:21
  36.5 7.8 %copy-start.25 = (bf16[32,64]{1,0:T(8,128)(2,1)S(1)}, bf16[32,64]{1,0:T(8,128)(2,1)}, u32[]{:S(2)}) copy-start(bf16[32,64]{1,0:T(8,128)(2,1)} %convert_reduce_fusion) | copy-start | bytes 12292
  48.3 5.7 collective-permute-start.4
  51.9 6.3 collective-permute-start.5
  58.3 6.9 copy-start.37
  58.3 9.1 %collective-permute-start.6 = (bf16[64,16,128]{2,1,0:T(8,128)(2,1)S(1)}, bf16[64,16,128]{2,1,0:T(8,128)(2,1)S(1)}, u32[]{:S(2)}, u32[]{:S(2)}) collective-permute-start(bf16[64,16,128]{2,1,0:T(8,128)(2,1)S(1)} %get-tuple-element.36), channel_id=1, source_target_pairs={{0,1},{1,2},{2,3},{3,4},{4,5},{5,6},{6,7},{7,8},{8,9},{9,10},{10,1... | collective-permute-start | bytes 786440 | tf_op jit(solution)/shard_map/ppermute | solution.py:19
  63.9 9.1 %collective-permute-start.7 = (bf16[64,16,128]{2,1,0:T(8,128)(2,1)S(1)}, bf16[64,16,128]{2,1,0:T(8,128)(2,1)S(1)}, u32[]{:S(2)}, u32[]{:S(2)}) collective-permute-start(bf16[64,16,128]{2,1,0:T(8,128)(2,1)S(1)} %get-tuple-element.37), channel_id=1, source_target_pairs={{1,0},{2,1},{3,2},{4,3},{5,4},{6,5},{7,6},{8,7},{9,8},{10,9},{11,1... | collective-permute-start | bytes 786440 | tf_op jit(solution)/shard_map/ppermute | solution.py:21
  66.7 6.4 copy-start.26
  110.8 2.5 copy-start.1
  113.2 113.9 %copy-start.7 = (bf16[2048,64]{1,0:T(8,128)(2,1)S(1)}, bf16[2048,64]{1,0:T(8,128)(2,1)}, u32[]{:S(2)}) copy-start(bf16[2048,64]{1,0:T(8,128)(2,1)} %reshape.269) | copy-start | bytes 786436
  228.1 5.5 copy-start.16
  229.2 8.9 %copy-start.5 = (bf16[2048,64]{1,0:T(8,128)(2,1)S(1)}, bf16[2048,64]{1,0:T(8,128)(2,1)}, u32[]{:S(2)}) copy-start(bf16[2048,64]{1,0:T(8,128)(2,1)} %reshape.266) | copy-start | bytes 786436
  229.2 9.8 %collective-permute-start.8 = (bf16[16,32,128]{2,1,0:T(8,128)(2,1)S(1)}, bf16[16,32,128]{2,1,0:T(8,128)(2,1)S(1)}, u32[]{:S(2)}, u32[]{:S(2)}) collective-permute-start(bf16[16,32,128]{2,1,0:T(8,128)(2,1)S(1)} %get-tuple-element.32), channel_id=1, source_target_pairs={{0,32},{32,64},{64,96},{96,128},{128,160},{160,192},{192,224},{224... | collective-permute-start | bytes 393224 | tf_op jit(solution)/shard_map/ppermute | solution.py:19
  231.3 7.8 %collective-permute-start.9 = (bf16[16,32,128]{2,1,0:T(8,128)(2,1)S(1)}, bf16[16,32,128]{2,1,0:T(8,128)(2,1)S(1)}, u32[]{:S(2)}, u32[]{:S(2)}) collective-permute-start(bf16[16,32,128]{2,1,0:T(8,128)(2,1)S(1)} %get-tuple-element.33), channel_id=1, source_target_pairs={{32,0},{64,32},{96,64},{128,96},{160,128},{192,160},{224,192},{256... | collective-permute-start | bytes 393224 | tf_op jit(solution)/shard_map/ppermute | solution.py:21
  233.7 6.1 collective-permute-start.10
  236.6 8.8 %collective-permute-start.11 = (bf16[32,16,128]{2,1,0:T(8,128)(2,1)S(1)}, bf16[32,16,128]{2,1,0:T(8,128)(2,1)S(1)}, u32[]{:S(2)}, u32[]{:S(2)}) collective-permute-start(bf16[32,16,128]{2,1,0:T(8,128)(2,1)S(1)} %get-tuple-element.35), channel_id=1, source_target_pairs={{1,0},{2,1},{3,2},{4,3},{5,4},{6,5},{7,6},{8,7},{9,8},{10,9},{11,1... | collective-permute-start | bytes 393224 | tf_op jit(solution)/shard_map/ppermute | solution.py:21
  239.2 6.4 copy-start.12
  249.1 1.7 copy-start.4
  254.4 433.7 %all-reduce.10.cloned.1.call-start = ((), (), s32[]{:S(2)}) async-start(), calls=%async_computation.1 | async-start | bytes 393216 | tf_op jit(solution)/shard_map/psum | solution.py:159
  255.0 5.1 copy-start.15
  255.1 286.3 %collective-permute-start.12 = (bf16[16,32,128]{2,1,0:T(8,128)(2,1)S(1)}, bf16[16,32,128]{2,1,0:T(8,128)(2,1)S(1)}, u32[]{:S(2)}, u32[]{:S(2)}) collective-permute-start(bf16[16,32,128]{2,1,0:T(8,128)(2,1)S(1)} %get-tuple-element.28), channel_id=1, source_target_pairs={{0,32},{32,64},{64,96},{96,128},{128,160},{160,192},{192,224},{224... | collective-permute-start | bytes 393224 | tf_op jit(solution)/shard_map/ppermute | solution.py:19
  258.2 283.1 %collective-permute-start.13 = (bf16[16,32,128]{2,1,0:T(8,128)(2,1)S(1)}, bf16[16,32,128]{2,1,0:T(8,128)(2,1)S(1)}, u32[]{:S(2)}, u32[]{:S(2)}) collective-permute-start(bf16[16,32,128]{2,1,0:T(8,128)(2,1)S(1)} %get-tuple-element.29), channel_id=1, source_target_pairs={{32,0},{64,32},{96,64},{128,96},{160,128},{192,160},{224,192},{256... | collective-permute-start | bytes 393224 | tf_op jit(solution)/shard_map/ppermute | solution.py:21
  260.8 280.7 %collective-permute-start.14 = (bf16[32,16,128]{2,1,0:T(8,128)(2,1)S(1)}, bf16[32,16,128]{2,1,0:T(8,128)(2,1)S(1)}, u32[]{:S(2)}, u32[]{:S(2)}) collective-permute-start(bf16[32,16,128]{2,1,0:T(8,128)(2,1)S(1)} %get-tuple-element.30), channel_id=1, source_target_pairs={{0,1},{1,2},{2,3},{3,4},{4,5},{5,6},{6,7},{7,8},{8,9},{9,10},{10,1... | collective-permute-start | bytes 393224 | tf_op jit(solution)/shard_map/ppermute | solution.py:19
  264.4 277.1 %collective-permute-start.15 = (bf16[32,16,128]{2,1,0:T(8,128)(2,1)S(1)}, bf16[32,16,128]{2,1,0:T(8,128)(2,1)S(1)}, u32[]{:S(2)}, u32[]{:S(2)}) collective-permute-start(bf16[32,16,128]{2,1,0:T(8,128)(2,1)S(1)} %get-tuple-element.31), channel_id=1, source_target_pairs={{1,0},{2,1},{3,2},{4,3},{5,4},{6,5},{7,6},{8,7},{9,8},{10,9},{11,1... | collective-permute-start | bytes 393224 | tf_op jit(solution)/shard_map/ppermute | solution.py:21
  (27 other events, 23.5 us)
Sparse Core Ops, SparseCore 0:
  254.5 286.7 all-reduce.7
  544.5 143.5 all-reduce.9
